TPU v7x, 256 devices: a whole 4x4x8 slice. The times are simulated.
256 devices in a mesh: dp: 4 (over x), space: 64 (over y, z, core).
Axes of the slice: x: 4, y: 4, z: 8, core: 2. Of those that a mesh axis runs over, the one named last changes fastest.
Arguments:
- features: bfloat16 [4, 64, 96, 1024], P('dp', 'space'), may hold values from -6 to 6
- cotangent: bfloat16 [4, 64, 192, 128], P('dp', 'space'), may hold values from -6 to 6
- conv_weight: bfloat16 [96, 2592], replicated, may hold values from -0.125 to 0.125
- down_weight: bfloat16 [192, 768], replicated, may hold values from -0.21875 to 0.21875
- neighbours: int32 [4, 64, 26], P('dp', 'space'), may hold values from -1 to 63, as said below
Outputs:
- coarse_out: bfloat16 [4, 64, 192, 128], P('dp', 'space')
- grad_features: float32 [4, 64, 96, 1024], P('dp', 'space')
- grad_conv: float32 [96, 2592], replicated
- grad_down: float32 [192, 768], replicated
Inputs may be any that keep to these rules, and one draw needn't show every extreme that they name: The blocks of a tile sit at distinct cells of a grid; if neighbours[t, s, d] = p is not -1 then neighbours[t, p, 25 - d] = s; a row never names its own block and names a device at most once.
All inputs are finite; a program needn't handle non-finite values.
Results may differ from a plain program's by a relative error of at most 0.0095.
Values may be sent and summed in bfloat16 or wider, within the bound.
No kernel may reach another device: no remote copies, remote signals or barrier semaphores. Data moves between devices by JAX's collectives and lax.ppermute only.
A program may use at most 128 MiB of HBM per device.

v0:
```python
import jax
import jax.numpy as jnp
from jax import lax
from jax.sharding import PartitionSpec as P

BRICK = 8
DIRECTIONS = [
    (step_x, step_y, step_z)
    for step_x in (-1, 0, 1)
    for step_y in (-1, 0, 1)
    for step_z in (-1, 0, 1)
    if (step_x, step_y, step_z) != (0, 0, 0)
]
EPSILON = 1e-06


def cut_inner(offset, extent):
    if offset < 0:
        return slice(0, 1)
    if offset > 0:
        return slice(extent - 1, extent)
    return slice(0, extent)


def cut_outer(offset, extent):
    if offset < 0:
        return slice(0, 1)
    if offset > 0:
        return slice(extent + 1, extent + 2)
    return slice(1, extent + 1)


def inner_layer(block_data, offset):
    return block_data[
        :,
        cut_inner(offset[0], block_data.shape[1]),
        cut_inner(offset[1], block_data.shape[2]),
        cut_inner(offset[2], block_data.shape[3]),
    ]


def outer_layer(padded, offset):
    return padded[
        :,
        cut_outer(offset[0], padded.shape[1] - 2),
        cut_outer(offset[1], padded.shape[2] - 2),
        cut_outer(offset[2], padded.shape[3] - 2),
    ]


def conv_taps(padded, weight_matrix):
    channels = padded.shape[0]
    size_x, size_y, size_z = (padded.shape[1] - 2, padded.shape[2] - 2, padded.shape[3] - 2)
    accumulated = jnp.zeros((weight_matrix.shape[0], size_x * size_y * size_z), jnp.float32)
    for step_x in range(3):
        for step_y in range(3):
            columns = jnp.concatenate(
                [
                    padded[
                        :,
                        step_x : step_x + size_x,
                        step_y : step_y + size_y,
                        step_z : step_z + size_z,
                    ]
                    for step_z in range(3)
                ],
                axis=0,
            ).reshape(3 * channels, size_x * size_y * size_z)
            start_col = (step_x * 3 + step_y) * 3 * channels
            accumulated = accumulated + jnp.dot(
                weight_matrix[:, start_col : start_col + 3 * channels],
                columns,
                preferred_element_type=jnp.float32,
            )
    return accumulated


def weight_taps(padded, grad_out):
    channels = padded.shape[0]
    size_x, size_y, size_z = (padded.shape[1] - 2, padded.shape[2] - 2, padded.shape[3] - 2)
    blocks_out = []
    for step_x in range(3):
        for step_y in range(3):
            columns = jnp.concatenate(
                [
                    padded[
                        :,
                        step_x : step_x + size_x,
                        step_y : step_y + size_y,
                        step_z : step_z + size_z,
                    ]
                    for step_z in range(3)
                ],
                axis=0,
            ).reshape(3 * channels, size_x * size_y * size_z)
            blocks_out.append(
                lax.dot_general(
                    grad_out, columns, (((1,), (1,)), ((), ())), preferred_element_type=jnp.float32
                )
            )
    return jnp.concatenate(blocks_out, axis=1)


def flipped(weight_matrix):
    channels = weight_matrix.shape[0]
    return (
        weight_matrix.reshape(channels, 27, channels)[:, ::-1, :]
        .transpose(2, 1, 0)
        .reshape(channels, 27 * channels)
    )


def coarse_patches(hidden_block):
    channels, size_x, size_y, size_z = hidden_block.shape
    split = hidden_block.reshape(channels, size_x // 2, 2, size_y // 2, 2, size_z // 2, 2)
    return split.transpose(2, 4, 6, 0, 1, 3, 5).reshape(
        8 * channels, size_x // 2 * (size_y // 2) * (size_z // 2)
    )


def from_patches(patch_data, channels, size_x, size_y, size_z):
    split = patch_data.reshape(2, 2, 2, channels, size_x // 2, size_y // 2, size_z // 2)
    return split.transpose(3, 4, 0, 5, 1, 6, 2).reshape(channels, size_x * size_y * size_z)


def silu_slope(activation):
    sigmoid_value = jax.nn.sigmoid(activation)
    return sigmoid_value * (1.0 + activation * (1.0 - sigmoid_value))


def normalized(accumulated):
    return accumulated * lax.rsqrt(jnp.mean(accumulated * accumulated) + EPSILON)


def shards(features, cotangent, conv_weight, down_weight, neighbours):
    channels = features.shape[2]
    block_side = BRICK
    block_depth = features.shape[3] // (block_side * block_side)
    peer_count = lax.axis_size("space")
    capacity = max(block_side * block_side, block_side * block_depth)
    owner_row = neighbours[0, 0]
    present = owner_row >= 0
    target = jnp.where(present, owner_row, peer_count)
    source = jnp.clip(owner_row, 0, peer_count - 1)

    def pack_faces(face_layers, wire_type):
        stacked = jnp.stack(
            [
                jnp.pad(
                    face_layer.reshape(channels, -1), ((0, 0), (0, capacity - face_layer[0].size))
                )
                for face_layer in face_layers
            ]
        )
        return (
            jnp.zeros((peer_count, channels, capacity), wire_type)
            .at[target]
            .set(stacked, mode="drop")
        )

    def unpack_faces(received, shapes):
        picked = jnp.take(received, source, axis=0) * present[:, None, None].astype(received.dtype)
        pieces = []
        for number, shape in enumerate(shapes):
            count = shape[1] * shape[2] * shape[3]
            pieces.append(picked[number, :, :count].reshape(shape))
        return pieces

    def fill_rim(block_data, received):
        padded = jnp.pad(block_data, ((0, 0), (1, 1), (1, 1), (1, 1)))
        pieces = unpack_faces(
            received, [inner_layer(block_data, offset).shape for offset in DIRECTIONS]
        )
        for offset, face_piece in zip(DIRECTIONS, pieces):
            padded = padded.at[
                :,
                cut_outer(offset[0], block_side),
                cut_outer(offset[1], block_side),
                cut_outer(offset[2], block_depth),
            ].set(face_piece)
        return padded

    own_block = features[0, 0].reshape(channels, block_side, block_side, block_depth)
    sent = pack_faces([inner_layer(own_block, offset) for offset in DIRECTIONS], jnp.bfloat16)
    received = lax.all_to_all(sent, "space", split_axis=0, concat_axis=0, tiled=True)
    padded = fill_rim(own_block, received)
    preact = conv_taps(padded, conv_weight)
    hidden = jax.nn.silu(preact).astype(jnp.bfloat16)
    patches = coarse_patches(hidden.reshape(channels, block_side, block_side, block_depth))
    coarse_out = jnp.dot(down_weight, patches, preferred_element_type=jnp.float32).astype(
        jnp.bfloat16
    )
    cot_block = cotangent[0, 0]
    down_part = lax.dot_general(
        cot_block, patches, (((1,), (1,)), ((), ())), preferred_element_type=jnp.float32
    )
    spread_back = from_patches(
        jnp.dot(down_weight.T, cot_block, preferred_element_type=jnp.float32),
        channels,
        block_side,
        block_side,
        block_depth,
    )
    grad_pre = (spread_back * silu_slope(preact)).astype(jnp.bfloat16)
    conv_part = weight_taps(padded, grad_pre)
    flip_weight = flipped(conv_weight)
    grad_block = grad_pre.reshape(channels, block_side, block_side, block_depth)
    widened = jnp.pad(grad_block, ((0, 0), (2, 2), (2, 2), (2, 2)))
    full_grad = conv_taps(widened, flip_weight).reshape(
        channels, block_side + 2, block_side + 2, block_depth + 2
    )
    spill_buffer = pack_faces(
        [outer_layer(full_grad, offset) for offset in DIRECTIONS], jnp.float32
    )
    got_spill = lax.all_to_all(
        spill_buffer.astype(jnp.bfloat16), "space", split_axis=0, concat_axis=0, tiled=True
    ).astype(spill_buffer.dtype)
    inner_part = full_grad[:, 1:-1, 1:-1, 1:-1]
    pieces = unpack_faces(
        got_spill, [inner_layer(inner_part, offset).shape for offset in DIRECTIONS]
    )
    for offset, face_piece in zip(DIRECTIONS, pieces):
        inner_part = inner_part.at[
            :,
            cut_inner(offset[0], block_side),
            cut_inner(offset[1], block_side),
            cut_inner(offset[2], block_depth),
        ].add(face_piece)
    grad_features = inner_part.reshape(channels, -1)
    conv_sum, down_sum = lax.psum((conv_part, down_part), ("dp", "space"))
    return (
        coarse_out[None, None],
        grad_features[None, None],
        normalized(conv_sum),
        normalized(down_sum),
    )


def solution(mesh):
    placed = (
        P("dp", "space", None, None),
        P("dp", "space", None, None),
        P(),
        P(),
        P("dp", "space", None),
    )
    return jax.shard_map(
        shards,
        mesh=mesh,
        in_specs=placed,
        out_specs=(P("dp", "space", None, None), P("dp", "space", None, None), P(), P()),
        check_vma=False,
    )
```

profile of v0, /device:TPU:2, one launch (start us, length us, event | category | flops | bytes accessed | tf_op | source)
XLA Modules:
  0.0 610.5 jit_solution(4286179501511224729)
XLA Ops:
  10.8 5.3 scatter_fusion
  16.1 12.1 %all-to-all-start = ((bf16[64,96,128]{2,1,0:T(8,128)(2,1)}), bf16[64,96,128]{2,1,0:T(8,128)(2,1)S(1)}, u32[]{:S(2)}, u32[]{:S(2)}) async-start(bf16[64,96,128]{2,1,0:T(8,128)(2,1)} %scatter_fusion), calls=%async_computation | async-start | bytes 3145728 | tf_op jit(solution)/shard_map/all_to_all | solution.py:185
  31.8 35.9 %all-to-all-done = bf16[64,96,128]{2,1,0:T(8,128)(2,1)S(1)} async-done(((bf16[64,96,128]{2,1,0:T(8,128)(2,1)}), bf16[64,96,128]{2,1,0:T(8,128)(2,1)S(1)}, u32[]{:S(2)}, u32[]{:S(2)}) %all-to-all-start) | async-done | bytes 1572896 | tf_op jit(solution)/shard_map/all_to_all | solution.py:185
  96.3 5.5 pad_slice_fusion.2
  127.2 2.6 pad_maximum_fusion.2
  154.9 3.7 scatter_fusion.1
  160.1 7.0 %all-to-all-start.1 = ((bf16[64,96,128]{2,1,0:T(8,128)(2,1)}), bf16[64,96,128]{2,1,0:T(8,128)(2,1)}, u32[]{:S(2)}, u32[]{:S(2)}) async-start(bf16[64,96,128]{2,1,0:T(8,128)(2,1)} %convert_element_type.100), calls=%async_computation.1 | async-start | bytes 3145728 | tf_op jit(solution)/shard_map/all_to_all | solution.py:215
  183.0 257.4 %all-reduce.49.cloned.1.call-done = (f32[96,2592]{1,0:T(8,128)}, f32[192,768]{1,0:T(8,128)}) async-done(((f32[96,2592]{1,0:T(8,128)}, f32[192,768]{1,0:T(8,128)}), (f32[96,2592]{1,0:T(8,128)}, f32[192,768]{1,0:T(8,128)})) %all-reduce.49.cloned.1.call-update) | async-done | bytes 1585168 | tf_op jit(solution)/shard_map/psum | solution.py:230
  448.8 3.5 convert_element_type.101
  452.3 3.6 gather_fusion.1
  469.1 2.6 scatter-add.91
  476.0 2.8 add_select_fusion.1
  478.8 4.6 scatter-add.95
  484.4 2.6 fusion.25
  491.7 3.0 scatter-add.101
  499.0 2.8 add_select_fusion
  501.8 4.8 scatter-add.105
  509.7 4.2 slice_add_fusion.1
  513.9 18.6 %scatter-add.106 = f32[96,8,8,16]{3,0,2,1:T(8,128)S(1)} dynamic-update-slice(f32[96,8,8,16]{3,0,2,1:T(8,128)S(1)} %scatter-add.105, f32[96,8,8,1]{3,0,2,1:T(8,128)} %slice_add_fusion.1, s32[]{:T(128)} %constant.1634.clone.1, s32[]{:T(128)} %constant.1634.clone.1, s32[]{:T(128)} %constant.1634.clone.1, s32[]{:T(128)} %constant.1634.clone.1) | dynamic-update-slice | bytes 49156 | tf_op jit(solution)/shard_map/scatter-add | solution.py:228
  534.9 4.4 slice_add_fusion
  539.3 23.3 %scatter-add.109 = f32[96,8,8,16]{3,0,2,1:T(8,128)S(1)} dynamic-update-slice(f32[96,8,8,16]{3,0,2,1:T(8,128)S(1)} %scatter-add.106, f32[96,8,8,1]{3,0,2,1:T(8,128)} %slice_add_fusion, s32[]{:T(128)} %constant.1634.clone.1, s32[]{:T(128)} %constant.1634.clone.1, s32[]{:T(128)} %constant.1634.clone.1, s32[]{:T(128)} %constant.1644.clone.1) | dynamic-update-slice | bytes 49156 | tf_op jit(solution)/shard_map/scatter-add | solution.py:228
  565.0 3.0 scatter-add.110
  573.9 3.6 scatter-add.114
  592.9 3.3 scatter-add.124
  (363 shorter events, 172.7 us)
Async XLA Ops:
  16.1 12.3 %copy-start.22 = (bf16[192,768]{1,0:T(8,128)(2,1)S(1)}, bf16[192,768]{1,0:T(8,128)(2,1)}, u32[]{:S(2)}) copy-start(bf16[192,768]{1,0:T(8,128)(2,1)} %param.112) | copy-start | bytes 884740
  16.1 12.5 %copy-start.32 = (bf16[1,1,192,128]{3,2,1,0:T(8,128)(2,1)S(1)}, bf16[1,1,192,128]{3,2,1,0:T(8,128)(2,1)}, u32[]{:S(2)}) copy-start(bf16[1,1,192,128]{3,2,1,0:T(8,128)(2,1)} %param.110) | copy-start | bytes 147460
  16.1 51.6 %all-to-all-start = ((bf16[64,96,128]{2,1,0:T(8,128)(2,1)}), bf16[64,96,128]{2,1,0:T(8,128)(2,1)S(1)}, u32[]{:S(2)}, u32[]{:S(2)}) async-start(bf16[64,96,128]{2,1,0:T(8,128)(2,1)} %scatter_fusion), calls=%async_computation | async-start | bytes 3145728 | tf_op jit(solution)/shard_map/all_to_all | solution.py:185
  28.6 1.8 copy-start.19
  75.3 3.2 copy-start
  77.1 3.2 copy-start.2
  78.9 3.2 copy-start.4
  80.7 3.1 copy-start.6
  87.6 1.8 copy-start.30
  140.2 2.1 copy-start.14
  140.2 2.1 copy-start.18
  160.1 7.1 %copy-start.7 = (bf16[288,8,8,16]{0,3,2,1:T(8,128)(2,1)S(1)}, bf16[288,8,8,16]{0,3,2,1:T(8,128)(2,1)}, u32[]{:S(2)}) copy-start(bf16[288,8,8,16]{0,3,2,1:T(8,128)(2,1)} %copy-done.6) | copy-start | bytes 1769476
  160.1 8.0 %copy-start.31 = (bf16[96,1024]{1,0:T(8,128)(2,1)S(1)}, bf16[96,1024]{1,0:T(8,128)(2,1)}, u32[]{:S(2)}) copy-start(bf16[96,1024]{1,0:T(8,128)(2,1)} %get-tuple-element.737) | copy-start | bytes 589828
  160.1 288.7 %all-to-all-start.1 = ((bf16[64,96,128]{2,1,0:T(8,128)(2,1)}), bf16[64,96,128]{2,1,0:T(8,128)(2,1)}, u32[]{:S(2)}, u32[]{:S(2)}) async-start(bf16[64,96,128]{2,1,0:T(8,128)(2,1)} %convert_element_type.100), calls=%async_computation.1 | async-start | bytes 3145728 | tf_op jit(solution)/shard_map/all_to_all | solution.py:215
  167.1 2.7 copy-start.3
  167.1 273.4 %all-reduce.49.cloned.1.call-start = ((), (), s32[]{:S(2)}) async-start(), calls=%async_computation.2 | async-start | bytes 3244032 | tf_op jit(solution)/shard_map/psum | solution.py:230
  168.3 1.8 copy-start.1
  170.1 2.0 copy-start.33
  172.1 2.3 copy-start.36
  172.1 3.1 copy-start.37
  172.1 3.1 copy-start.38
  445.8 2.0 copy-start.16
  513.9 18.6 %copy-start.35 = (f32[1,96,64]{2,1,0:T(8,128)S(1)}, f32[1,96,64]{2,1,0:T(8,128)}, u32[]{:S(2)}) copy-start(f32[1,96,64]{2,1,0:T(8,128)} %get-tuple-element.662) | copy-start | bytes 73732
  539.3 23.3 %copy-start.34 = (f32[96,8,1,1]{1,0,3,2:T(8,128)S(1)}, f32[96,8,1,1]{1,0,3,2:T(8,128)}, u32[]{:S(2)}) copy-start(f32[96,8,1,1]{1,0,3,2:T(8,128)} %get-tuple-element.653) | copy-start | bytes 9220
  (19 other events, 25.1 us)
Sparse Core Ops, SparseCore 0:
  174.0 266.4 all-reduce.48
where the time goes:
time: 620 us; the launch traced here: 610 us
  waiting for transfers between devices  293 us (47%)
  local copies, waits for them, and re-layouts  177 us (29%)
  other arithmetic  73.2 us (12%)
  matrix products  29.7 us (5%)
  starting transfers between devices  19.2 us (3%)
  between operations  17.5 us (3%)
    psum x1, waiting for transfers between devices, shards(): conv_sum, down_sum = lax.psum((conv_part, down_part), ('dp', 'space'))  257 us
    scatter-add x22, local copies, waits for them, and re-layouts, shards(): inner_part = inner_part.at[:, cut_inner(offset[0], block_side), cut_inner...  75.3 us
    all_to_all x1, waiting for transfers between devices, shards(): lax.all_to_all(sent, 'space', split_axis=0, concat_axis=0, tiled=True)  35.9 us
    another operation x33, local copies, waits for them, and re-layouts  26 us
    concatenate x18, other arithmetic, conv_taps(): jnp.concatenate([padded[:, step_x:step_x + size_x, step_y:step_y + size_y...  24 us
    add x19, other arithmetic, shards(): inner_part = inner_part.at[:, cut_inner(offset[0], block_side), cut_inner...  22.2 us
    dot_general x18, matrix products, conv_taps(): jnp.dot(weight_matrix[:, start_col:start_col + 3 * channels], columns, pr...  19.3 us
    reshape x9, local copies, waits for them, and re-layouts, conv_taps(): columns = jnp.concatenate([padded[:, step_x:step_x + size_x, step_y:step_...  15.8 us
  transfers between devices with their start and end apart: 3, of which 2 were waited for; matrix products, arithmetic and copies ran while one was open for 4% of the time, Pallas kernels for 0%

commit v1 on v0

--- a/solution.py
+++ b/solution.py
@@ -227,7 +227,7 @@
             cut_inner(offset[2], block_depth),
         ].add(face_piece)
     grad_features = inner_part.reshape(channels, -1)
-    conv_sum, down_sum = lax.psum((conv_part, down_part), ("dp", "space"))
+    conv_sum, down_sum = lax.psum(lax.psum((conv_part, down_part), "space"), "dp")
     return (
         coarse_out[None, None],
         grad_features[None, None],

time: 620 us -> 598 us (0.965)
  waiting for transfers between devices: 293 us -> 262 us
  local copies, waits for them, and re-layouts: 177 us -> 184 us
    psum x1 -> x2, waiting for transfers between devices: 257 us -> 226 us  [the longest x1 182 us: shards(): lax.psum((conv_part, down_part), 'space')]
    unnamed x141 -> x171, local copies, waits for them, and re-layouts: 14.3 us -> 15.2 us
  transfers between devices with their start and end apart: 3 -> 4, of which waited for: 2 -> 3; matrix products, arithmetic and copies ran while one was open for 4% -> 5% of each run, Pallas kernels for 0% -> 0%
where the time goes in v1:
time: 598 us; the launch traced here: 587 us
  waiting for transfers between devices  262 us (44%)
  local copies, waits for them, and re-layouts  184 us (31%)
  other arithmetic  74.2 us (12%)
  matrix products  30 us (5%)
  starting transfers between devices  19 us (3%)
  between operations  17.6 us (3%)
    psum x1, waiting for transfers between devices, shards(): lax.psum((conv_part, down_part), 'space')  182 us
    scatter-add x22, local copies, waits for them, and re-layouts, shards(): inner_part = inner_part.at[:, cut_inner(offset[0], block_side), cut_inner...  75.3 us
    psum x1, waiting for transfers between devices, shards(): lax.psum(lax.psum((conv_part, down_part), 'space'), 'dp')  44.4 us
    all_to_all x1, waiting for transfers between devices, shards(): lax.all_to_all(sent, 'space', split_axis=0, concat_axis=0, tiled=True)  35.3 us
    another operation x33, local copies, waits for them, and re-layouts  26.1 us
    concatenate x18, other arithmetic, conv_taps(): jnp.concatenate([padded[:, step_x:step_x + size_x, step_y:step_y + size_y...  24 us
    add x19, other arithmetic, shards(): inner_part = inner_part.at[:, cut_inner(offset[0], block_side), cut_inner...  22.2 us
    dot_general x18, matrix products, conv_taps(): jnp.dot(weight_matrix[:, start_col:start_col + 3 * channels], columns, pr...  18.9 us
  transfers between devices with their start and end apart: 4, of which 3 were waited for; matrix products, arithmetic and copies ran while one was open for 5% of the time, Pallas kernels for 0%

profile of v1, /device:TPU:2, one launch (start us, length us, event | category | flops | bytes accessed | tf_op | source)
XLA Modules:
  0.0 586.6 jit_solution(12996974185497361109)
XLA Ops:
  10.8 5.3 scatter_fusion
  16.1 12.1 %all-to-all-start = ((bf16[64,96,128]{2,1,0:T(8,128)(2,1)}), bf16[64,96,128]{2,1,0:T(8,128)(2,1)S(1)}, u32[]{:S(2)}, u32[]{:S(2)}) async-start(bf16[64,96,128]{2,1,0:T(8,128)(2,1)} %scatter_fusion), calls=%async_computation | async-start | bytes 3145728 | tf_op jit(solution)/shard_map/all_to_all | solution.py:185
  32.4 35.3 %all-to-all-done = bf16[64,96,128]{2,1,0:T(8,128)(2,1)S(1)} async-done(((bf16[64,96,128]{2,1,0:T(8,128)(2,1)}), bf16[64,96,128]{2,1,0:T(8,128)(2,1)S(1)}, u32[]{:S(2)}, u32[]{:S(2)}) %all-to-all-start) | async-done | bytes 1572896 | tf_op jit(solution)/shard_map/all_to_all | solution.py:185
  99.0 5.5 pad_slice_fusion.2
  130.0 2.6 pad_maximum_fusion.2
  167.5 3.9 scatter_fusion.1
  172.8 6.8 %all-to-all-start.1 = ((bf16[64,96,128]{2,1,0:T(8,128)(2,1)}), bf16[64,96,128]{2,1,0:T(8,128)(2,1)}, u32[]{:S(2)}, u32[]{:S(2)}) async-start(bf16[64,96,128]{2,1,0:T(8,128)(2,1)} %convert_element_type.100), calls=%async_computation.1 | async-start | bytes 3145728 | tf_op jit(solution)/shard_map/all_to_all | solution.py:215
  179.7 182.0 %all-reduce.51.cloned.1.call-done = (f32[96,2592]{1,0:T(8,128)}, f32[192,768]{1,0:T(8,128)}) async-done(((f32[96,2592]{1,0:T(8,128)}, f32[192,768]{1,0:T(8,128)}), (f32[96,2592]{1,0:T(8,128)}, f32[192,768]{1,0:T(8,128)})) %all-reduce.51.cloned.1.call-update) | async-done | bytes 1585168 | tf_op jit(solution)/shard_map/psum | solution.py:230
  371.7 44.4 %all-reduce.53.cloned.1.call-done = (f32[96,2592]{1,0:T(8,128)}, f32[192,768]{1,0:T(8,128)}) async-done(((f32[96,2592]{1,0:T(8,128)}, f32[192,768]{1,0:T(8,128)}), (f32[96,2592]{1,0:T(8,128)}, f32[192,768]{1,0:T(8,128)})) %all-reduce.53.cloned.1.call-update) | async-done | bytes 1585168 | tf_op jit(solution)/shard_map/psum | solution.py:230
  424.5 3.5 convert_element_type.101
  428.0 3.7 gather_fusion.1
  451.9 2.9 add_select_fusion.1
  454.8 4.7 scatter-add.95
  460.5 2.8 fusion.25
  467.7 3.2 scatter-add.101
  475.3 2.9 add_select_fusion
  478.1 4.9 scatter-add.105
  486.2 4.2 slice_add_fusion.1
  490.3 18.6 %scatter-add.106 = f32[96,8,8,16]{3,0,2,1:T(8,128)S(1)} dynamic-update-slice(f32[96,8,8,16]{3,0,2,1:T(8,128)S(1)} %scatter-add.105, f32[96,8,8,1]{3,0,2,1:T(8,128)} %slice_add_fusion.1, s32[]{:T(128)} %constant.1634.clone.1, s32[]{:T(128)} %constant.1634.clone.1, s32[]{:T(128)} %constant.1634.clone.1, s32[]{:T(128)} %constant.1634.clone.1) | dynamic-update-slice | bytes 49156 | tf_op jit(solution)/shard_map/scatter-add | solution.py:228
  511.3 4.5 slice_add_fusion
  515.8 23.3 %scatter-add.109 = f32[96,8,8,16]{3,0,2,1:T(8,128)S(1)} dynamic-update-slice(f32[96,8,8,16]{3,0,2,1:T(8,128)S(1)} %scatter-add.106, f32[96,8,8,1]{3,0,2,1:T(8,128)} %slice_add_fusion, s32[]{:T(128)} %constant.1634.clone.1, s32[]{:T(128)} %constant.1634.clone.1, s32[]{:T(128)} %constant.1634.clone.1, s32[]{:T(128)} %constant.1644.clone.1) | dynamic-update-slice | bytes 49156 | tf_op jit(solution)/shard_map/scatter-add | solution.py:228
  541.5 3.0 scatter-add.110
  550.4 3.6 scatter-add.114
  569.1 3.3 scatter-add.124
  (396 shorter events, 182.0 us)
Async XLA Ops:
  9.4 6.7 %copy-start.40 = (s32[26]{0:T(128)}, s32[26]{0:T(128)S(1)}, u32[]{:S(2)}) copy-start(s32[26]{0:T(128)S(1)} %get-tuple-element.800) | copy-start | bytes 316
  16.1 12.3 %copy-start.14 = (bf16[192,768]{1,0:T(8,128)(2,1)S(1)}, bf16[192,768]{1,0:T(8,128)(2,1)}, u32[]{:S(2)}) copy-start(bf16[192,768]{1,0:T(8,128)(2,1)} %param.112) | copy-start | bytes 884740
  16.1 12.5 %copy-start.20 = (bf16[1,1,192,128]{3,2,1,0:T(8,128)(2,1)S(1)}, bf16[1,1,192,128]{3,2,1,0:T(8,128)(2,1)}, u32[]{:S(2)}) copy-start(bf16[1,1,192,128]{3,2,1,0:T(8,128)(2,1)} %param.110) | copy-start | bytes 147460
  16.1 51.6 %all-to-all-start = ((bf16[64,96,128]{2,1,0:T(8,128)(2,1)}), bf16[64,96,128]{2,1,0:T(8,128)(2,1)S(1)}, u32[]{:S(2)}, u32[]{:S(2)}) async-start(bf16[64,96,128]{2,1,0:T(8,128)(2,1)} %scatter_fusion), calls=%async_computation | async-start | bytes 3145728 | tf_op jit(solution)/shard_map/all_to_all | solution.py:185
  28.2 333.5 %all-reduce.51.cloned.1.call-start = ((), (), s32[]{:S(2)}) async-start(), calls=%async_computation.2 | async-start | bytes 3244032 | tf_op jit(solution)/shard_map/psum | solution.py:230
  31.8 36.9 %copy-start.37 = (s32[1024]{0:T(1024)}, s32[1024]{0:T(1024)S(1)}, u32[]{:S(2)}) copy-start(s32[1024]{0:T(1024)S(1)} %pad_clamp_fusion) | copy-start | bytes 12292
  31.9 36.9 %copy-start.38 = (pred[26]{0:T(512)(128)(4,1)}, pred[26]{0:T(512)(128)(4,1)S(1)}, u32[]{:S(2)}) copy-start(pred[26]{0:T(512)(128)(4,1)S(1)} %compare_and_fusion) | copy-start | bytes 82
  143.0 2.1 copy-start.6
  143.0 2.1 copy-start.10
  154.6 4.5 copy-start.19
  154.6 5.2 copy-start.21
  154.7 9.1 %copy-start.9 = (f32[96,10,10,18]{0,3,2,1:T(8,128)}, f32[96,10,10,18]{0,3,2,1:T(8,128)S(1)}, u32[]{:S(2)}) copy-start(f32[96,10,10,18]{0,3,2,1:T(8,128)S(1)} %reshape.2481) | copy-start | bytes 2073604
  154.7 6.8 %copy-start.15 = (f32[96,288]{1,0:T(8,128)S(1)}, f32[96,288]{1,0:T(8,128)}, u32[]{:S(2)}) copy-start(f32[96,288]{1,0:T(8,128)} %fusion.71) | copy-start | bytes 331780
  172.8 190.2 %copy-start.51 = (s32[4]{0:T(128)S(1)}, s32[4]{0:T(128)}, u32[]{:S(2)}) copy-start(s32[4]{0:T(128)} %constant.1649.clone.1) | copy-start | bytes 52
  172.8 191.0 %copy-start.52 = (s32[4]{0:T(128)S(1)}, s32[4]{0:T(128)}, u32[]{:S(2)}) copy-start(s32[4]{0:T(128)} %constant.1646.clone.1) | copy-start | bytes 52
  172.8 191.0 %copy-start.53 = (s32[4]{0:T(128)S(1)}, s32[4]{0:T(128)}, u32[]{:S(2)}) copy-start(s32[4]{0:T(128)} %constant.1650.clone.1) | copy-start | bytes 52
  172.8 251.6 %all-to-all-start.1 = ((bf16[64,96,128]{2,1,0:T(8,128)(2,1)}), bf16[64,96,128]{2,1,0:T(8,128)(2,1)}, u32[]{:S(2)}, u32[]{:S(2)}) async-start(bf16[64,96,128]{2,1,0:T(8,128)(2,1)} %convert_element_type.100), calls=%async_computation.1 | async-start | bytes 3145728 | tf_op jit(solution)/shard_map/all_to_all | solution.py:215
  179.6 188.2 %copy-start.42 = (f32[96,1,1,1]{0,3,2,1:T(1,128)S(1)}, f32[96,1,1,1]{0,3,2,1:T(1,128)}, u32[]{:S(2)}) copy-start(f32[96,1,1,1]{0,3,2,1:T(1,128)} %get-tuple-element.667) | copy-start | bytes 1156
  179.6 236.5 %all-reduce.53.cloned.1.call-start = ((), (), s32[]{:S(2)}) async-start(), calls=%async_computation.3 | async-start | bytes 3244032 | tf_op jit(solution)/shard_map/psum | solution.py:230
  421.4 2.0 copy-start.8
  428.0 3.7 copy-start.39
  428.0 3.7 copy-start.50
  490.3 18.6 %copy-start.23 = (f32[1,96,64]{2,1,0:T(8,128)S(1)}, f32[1,96,64]{2,1,0:T(8,128)}, u32[]{:S(2)}) copy-start(f32[1,96,64]{2,1,0:T(8,128)} %get-tuple-element.664) | copy-start | bytes 73732
  515.8 23.3 %copy-start.22 = (f32[96,8,1,1]{1,0,3,2:T(8,128)S(1)}, f32[96,8,1,1]{1,0,3,2:T(8,128)}, u32[]{:S(2)}) copy-start(f32[96,8,1,1]{1,0,3,2:T(8,128)} %get-tuple-element.655) | copy-start | bytes 9220
  (35 other events, 40.6 us)
Sparse Core Ops, SparseCore 0:
  164.1 197.5 all-reduce.50
  364.1 51.9 all-reduce.52
